TPU v7x, 32 devices: a whole 2x2x4 slice. The times are simulated.
32 devices in a mesh: dp: 4 (over y, core), mp: 8 (over z, x).
Axes of the slice: x: 2, y: 2, z: 4, core: 2. Of those that a mesh axis runs over, the one named last changes fastest.
Arguments:
- query_rows: bfloat16 [8192, 16, 128], P('dp', 'mp'), may hold values from -8 to 8
- key_rows: bfloat16 [8192, 16, 128], P('dp', 'mp'), may hold values from -8 to 8
- value_rows: bfloat16 [8192, 16, 128], P('dp', 'mp'), may hold values from -6 to 6
- residual: bfloat16 [4096, 8, 768], P('dp', 'mp'), may hold values from -40 to 40
- lengths: int32 [64], replicated, may hold values from 1 to 256, as said below
- assignment: int32 [64], replicated, may hold values from 0 to 3, as said below
- out_proj: bfloat16 [1024, 1536], P(None, 'mp'), may hold values from -0.1875 to 0.1875
- norm_gain: float32 [1536], replicated, may hold values from 0.5 to 1.5
- norm_bias: float32 [1536], replicated, may hold values from -3 to 3
- glu_proj: bfloat16 [1536, 3072], P(None, 'mp'), may hold values from -0.15625 to 0.15625
- conv_taps: float32 [31, 1536], replicated, may hold values from -1 to 1
- batch_scale: float32 [1536], replicated, may hold values from 0.25 to 1.75
- batch_shift: float32 [1536], replicated, may hold values from -3 to 3
- down_proj: bfloat16 [1536, 1536], P(None, 'mp'), may hold values from -0.15625 to 0.15625
Outputs:
- encoded: bfloat16 [16384, 1536], P(('dp', 'mp'))
Inputs may be any that keep to these rules, and one draw needn't show every extreme that they name: `lengths`: utterance u starts in data group u // 16; a data group holds its utterances in order of u from its first frame on, and its frames after them are padding. In every draw every data group sends exactly 256 frames in each of its 4 utterances to one and the same data group, so that this group receives 4 * 256 frames from every data group; the utterances one data group sends to one data group never have more frames together. `assignment`: every data group sends exactly 4 of its utterances to each data group, itself included. In its new group an utterance lies after those of lower number, from the first frame on, and the frames after them are padding.
All inputs are finite; a program needn't handle non-finite values.
Results may differ from a plain program's by a relative error of at most 0.0034.
Values may be sent and summed in bfloat16 or wider, within the bound.
A program may use at most 128 MiB of HBM per device.

v0:
```python
import jax
import jax.numpy as jnp
from jax import lax
from jax.sharding import PartitionSpec as P

HD = 64
KERNEL = 31
HALF = 15
MAXLEN = 256
PIECES = 4
QBLK = 512
EPS = 1e-05
MASKED = -1e30


def with_halo(cells, sides, width):
    for axis, dim in sides:
        count = lax.axis_size(axis)
        ends = count - 1
        head = lax.slice_in_dim(cells, 0, width, axis=dim)
        tail = lax.slice_in_dim(cells, cells.shape[dim] - width, cells.shape[dim], axis=dim)
        cells = jnp.concatenate(
            [
                lax.ppermute(tail, axis, [(i, (i + 1) % count) for i in range(ends)]),
                cells,
                lax.ppermute(head, axis, [((i + 1) % count, i) for i in range(ends)]),
            ],
            axis=dim,
        )
    return cells


def unpack_pairs(packed):
    pair_rows, head_count, pair_width = packed.shape
    width = pair_width // 2
    return (
        packed.reshape(pair_rows, head_count, 2, width)
        .transpose(0, 2, 1, 3)
        .reshape(pair_rows * 2, head_count * width)
    )


def unpack_fours(packed):
    four_rows, block_count, four_width = packed.shape
    width = four_width // 4
    return (
        packed.reshape(four_rows, block_count, 4, width)
        .transpose(0, 2, 1, 3)
        .reshape(four_rows * 4, block_count * width)
    )


def utterance_tables(lengths, assignment, per_group):
    utterance_count = lengths.shape[0]
    utterance = jnp.arange(utterance_count, dtype=jnp.int32)
    source = utterance // per_group
    earlier = utterance[None, :] < utterance[:, None]
    same_source = source[None, :] == source[:, None]
    same_target = assignment[None, :] == assignment[:, None]
    span_table = jnp.broadcast_to(lengths[None, :], (utterance_count, utterance_count))
    nothing = jnp.zeros_like(span_table)
    before_start = jnp.sum(jnp.where(earlier & same_source, span_table, nothing), axis=1)
    after_start = jnp.sum(jnp.where(earlier & same_target, span_table, nothing), axis=1)
    slot_first = jnp.sum(
        jnp.where(earlier & same_source & same_target, span_table, nothing), axis=1
    )
    return (source, before_start, after_start, slot_first)


def find_frames(data_group, owner_group, first_frame, lengths, frames, lookup):
    position = jnp.arange(frames, dtype=jnp.int32)[:, None]
    matches = (
        (owner_group[None, :] == data_group)
        & (position >= first_frame[None, :])
        & (position < first_frame[None, :] + lengths[None, :])
    )
    utterance = jnp.arange(lengths.shape[0], dtype=jnp.int32)[None, :]
    occupied_slots = jnp.any(matches, axis=1)
    segment = jnp.where(occupied_slots, jnp.sum(jnp.where(matches, utterance, 0), axis=1), -1)
    shifted = jnp.sum(jnp.where(matches, lookup[None, :] - first_frame[None, :], 0), axis=1)
    source_row = jnp.where(occupied_slots, jnp.arange(frames, dtype=jnp.int32) + shifted, 0)
    return (segment, occupied_slots, source_row)


def outgoing_rows(
    data_group, groups, per_group, capacity, lengths, assignment, before_start, slot_first
):
    first_id = data_group * per_group
    own_length = lax.dynamic_slice_in_dim(lengths, first_id, per_group)
    own_target = lax.dynamic_slice_in_dim(assignment, first_id, per_group)
    own_before = lax.dynamic_slice_in_dim(before_start, first_id, per_group)
    own_slot = lax.dynamic_slice_in_dim(slot_first, first_id, per_group)
    slot_index = jnp.arange(groups * capacity, dtype=jnp.int32)
    target = (slot_index // capacity)[:, None]
    slot_place = (slot_index % capacity)[:, None]
    matches = (
        (own_target[None, :] == target)
        & (slot_place >= own_slot[None, :])
        & (slot_place < own_slot[None, :] + own_length[None, :])
    )
    valid_slot = jnp.any(matches, axis=1)
    send_frame = jnp.sum(
        jnp.where(matches, own_before[None, :] - own_slot[None, :] + slot_place, 0), axis=1
    )
    return (send_frame, valid_slot)


def pack_outgoing(stacked, send_frame, valid_slot):
    picked = jnp.take(stacked, send_frame, axis=0)
    return jnp.where(valid_slot[:, None], picked, jnp.zeros((), stacked.dtype))


def finalize_rows(received_rows, occupied_slots, incoming_row):
    picked = jnp.take(received_rows, incoming_row, axis=0)
    return jnp.where(occupied_slots[:, None], picked, jnp.zeros((), received_rows.dtype))


def attend(query_rows, key_rows, value_rows, segment, live_count):
    group_rows, width_per_head = query_rows.shape
    head_count = width_per_head // HD
    window = QBLK + 2 * MAXLEN
    score_scale = HD ** (-0.5)
    queries = query_rows.reshape(group_rows, head_count, HD)
    keyset = key_rows.reshape(group_rows, head_count, HD)
    valueset = value_rows.reshape(group_rows, head_count, HD)

    def attend_block(block_index, context):
        first_row = (block_index * QBLK).astype(jnp.int32)
        window_low = jnp.clip(first_row - MAXLEN, 0, group_rows - window)
        query_block = lax.dynamic_slice_in_dim(queries, first_row, QBLK, 0)
        key_block = lax.dynamic_slice_in_dim(keyset, window_low, window, 0)
        value_block = lax.dynamic_slice_in_dim(valueset, window_low, window, 0)
        segment_query = lax.dynamic_slice_in_dim(segment, first_row, QBLK, 0)
        segment_key = lax.dynamic_slice_in_dim(segment, window_low, window, 0)
        allowed = (segment_query[:, None] == segment_key[None, :]) & (segment_key[None, :] >= 0)
        scores = (
            jnp.einsum("qhd,khd->hqk", query_block, key_block, preferred_element_type=jnp.float32)
            * score_scale
        )
        scores = jnp.where(allowed[None], scores, MASKED)
        highest = jnp.max(scores, axis=2, keepdims=True)
        exponentials = jnp.exp(scores - highest)
        denominator = jnp.sum(exponentials, axis=2, keepdims=True)
        weights = (exponentials / denominator).astype(jnp.bfloat16)
        blended = jnp.einsum(
            "hqk,khd->qhd", weights, value_block, preferred_element_type=jnp.float32
        )
        blended = jnp.where((segment_query >= 0)[:, None, None], blended, 0.0).astype(jnp.bfloat16)
        return lax.dynamic_update_slice_in_dim(
            context, blended.reshape(QBLK, width_per_head), first_row, 0
        )

    blocks = (live_count + QBLK - 1) // QBLK
    return lax.fori_loop(
        0, blocks, attend_block, jnp.zeros((group_rows, width_per_head), jnp.bfloat16)
    )


def front(context_rows, carried_rows, out_proj, norm_gain, norm_bias, glu_proj):
    carried = carried_rows.astype(jnp.float32) + jnp.dot(
        context_rows,
        lax.all_gather(out_proj, "mp", axis=1, tiled=True),
        preferred_element_type=jnp.float32,
    )
    average = jnp.mean(carried, axis=1, keepdims=True)
    centred = carried - average
    variance = jnp.mean(centred * centred, axis=1, keepdims=True)
    normed = (centred * lax.rsqrt(variance + EPS) * norm_gain + norm_bias).astype(jnp.bfloat16)
    halves = jnp.dot(
        normed,
        lax.all_gather(glu_proj, "mp", axis=1, tiled=True),
        preferred_element_type=jnp.float32,
    )
    feature_count = halves.shape[1] // 2
    gated_rows = (halves[:, :feature_count] * jax.nn.sigmoid(halves[:, feature_count:])).astype(
        jnp.bfloat16
    )
    return (carried, gated_rows)


def depthwise(gated_rows, segment, conv_taps):
    output_rows = gated_rows.shape[0] - 2 * HALF
    centre = segment[HALF : HALF + output_rows]
    accumulated = jnp.zeros((output_rows, gated_rows.shape[1]), jnp.float32)
    for tap_index in range(KERNEL):
        same_segment = (segment[tap_index : tap_index + output_rows] == centre)[:, None]
        term = jnp.where(
            same_segment, gated_rows[tap_index : tap_index + output_rows].astype(jnp.float32), 0.0
        )
        accumulated = accumulated + term * conv_taps[tap_index]
    return accumulated


def on_device(
    query_rows,
    key_rows,
    value_rows,
    residual,
    lengths,
    assignment,
    out_proj,
    norm_gain,
    norm_bias,
    glu_proj,
    conv_taps,
    batch_scale,
    batch_shift,
    down_proj,
):
    query_flat = unpack_pairs(query_rows)
    key_flat = unpack_pairs(key_rows)
    value_flat = unpack_pairs(value_rows)
    residual_flat = unpack_fours(residual)
    data_group = lax.axis_index("dp")
    slab_index = lax.axis_index("mp")
    groups = lax.axis_size("dp")
    slab_count = lax.axis_size("mp")
    group_rows = query_flat.shape[0]
    slab_rows = group_rows // slab_count
    width_per_head = query_flat.shape[1]
    per_group = lengths.shape[0] // groups
    capacity = PIECES * MAXLEN
    source, before_start, after_start, slot_first = utterance_tables(lengths, assignment, per_group)
    receive_table = source * capacity + slot_first
    segment, occupied_slots, incoming_row = find_frames(
        data_group, assignment, after_start, lengths, group_rows, receive_table
    )
    send_frame, valid_slot = outgoing_rows(
        data_group, groups, per_group, capacity, lengths, assignment, before_start, slot_first
    )
    padded_segment = jnp.pad(segment, (HALF, HALF), constant_values=-2)
    wide_segment = lax.dynamic_slice_in_dim(
        padded_segment, slab_index * slab_rows, slab_rows + 2 * HALF
    )
    centre_segment = wide_segment[HALF : HALF + slab_rows]
    members = [query_flat, key_flat, value_flat, residual_flat]
    stacked = jnp.concatenate(members, axis=1)
    received_rows = lax.all_to_all(
        pack_outgoing(stacked, send_frame, valid_slot),
        "dp",
        split_axis=0,
        concat_axis=0,
        tiled=True,
    )
    balanced_rows = finalize_rows(received_rows, occupied_slots, incoming_row)
    context = attend(
        balanced_rows[:, :width_per_head],
        balanced_rows[:, width_per_head : 2 * width_per_head],
        balanced_rows[:, 2 * width_per_head : 3 * width_per_head],
        segment,
        jnp.sum(occupied_slots.astype(jnp.int32)),
    )
    portion_carried = balanced_rows[:, 3 * width_per_head :]
    context_slab, carried_slab = (
        lax.all_to_all(context, "mp", split_axis=0, concat_axis=1, tiled=True),
        lax.all_to_all(portion_carried, "mp", split_axis=0, concat_axis=1, tiled=True),
    )
    carried, gated_rows = front(
        context_slab, carried_slab, out_proj, norm_gain, norm_bias, glu_proj
    )
    wide_gated = with_halo(gated_rows, (("mp", 0),), HALF)
    convolved = depthwise(wide_gated, wide_segment, conv_taps)
    affine = convolved * batch_scale + batch_shift
    swished = (affine * jax.nn.sigmoid(affine)).astype(jnp.bfloat16)
    lowered = jnp.dot(
        swished,
        lax.all_gather(down_proj, "mp", axis=1, tiled=True),
        preferred_element_type=jnp.float32,
    )
    return jnp.where((centre_segment >= 0)[:, None], carried + lowered, 0.0).astype(jnp.bfloat16)


def solution(mesh):
    in_specs = (
        P("dp", "mp", None),
        P("dp", "mp", None),
        P("dp", "mp", None),
        P("dp", "mp", None),
        P(),
        P(),
        P(None, "mp"),
        P(),
        P(),
        P(None, "mp"),
        P(),
        P(),
        P(),
        P(None, "mp"),
    )
    out_specs = P(("dp", "mp"), None)
    return jax.shard_map(
        on_device, mesh=mesh, in_specs=in_specs, out_specs=out_specs, check_vma=False
    )
```

profile of v0, /device:TPU:4, one launch (start us, length us, event | category | flops | bytes accessed | tf_op | source)
XLA Modules:
  0.0 453.2 jit_solution(10994633186165721107)
XLA Ops:
  8.0 2.4 copy.61
  10.5 1.5 copy.62
  13.0 3.7 copy.63
  16.7 4.5 %copy.64 = bf16[2048,2,2,64]{3,2,1,0:T(2,128)(2,1)S(1)} copy(bf16[2048,2,2,64]{0,3,1,2:T(8,128)(2,1)} %bitcast.38) | data formatting | bytes 2097152 | tf_op jit(solution)/shard_map/transpose | solution.py:38
  21.2 1.8 reshape.219
  23.0 3.7 copy.65
  26.7 4.5 copy.66
  31.2 1.8 reshape.221
  33.0 3.6 reshape_transpose_reshape.3
  37.2 4.5 pad_maximum_fusion
  41.7 21.2 %gather_fusion = bf16[4096,576]{1,0:T(8,128)(2,1)} fusion(bf16[4096,576]{1,0:T(8,128)(2,1)} %pad_maximum_fusion, s32[4096]{0:T(1024)S(1)} %fusion.80), kind=kCustom, calls=%fused_computation.clone | custom fusion | bytes 9453568 | tf_op jit(solution)/shard_map/jit(_take)/gather | solution.py:109
  63.0 5.8 %select_select_fusion.1 = bf16[4096,576]{1,0:T(8,128)(2,1)} fusion(bf16[4096,576]{1,0:T(8,128)(2,1)} %gather_fusion, pred[4096]{0:T(1024)(128)(4,1)S(1)} %compare_and_fusion.5, pred[4096]{0:T(1024)(128)(4,1)S(1)} %fusion.85), kind=kLoop, calls=%fused_computation.59 | loop fusion | flops 4718592 | bytes 9445376 | tf_op jit(solution)/shard_map/jit(_where)/select_n | solution.py:110
  68.9 7.7 %copy.67 = bf16[4,1024,576]{1,2,0:T(8,128)(2,1)} copy(bf16[4,1024,576]{2,1,0:T(8,128)(2,1)} %bitcast.35) | data formatting | bytes 9437184 | tf_op jit(solution)/shard_map/all_to_all | solution.py:238
  76.5 5.1 %all-to-all-start = ((bf16[4,1024,576]{1,2,0:T(8,128)(2,1)}), bf16[4,1024,576]{1,2,0:T(8,128)(2,1)}, u32[]{:S(2)}, u32[]{:S(2)}) async-start(bf16[4,1024,576]{1,2,0:T(8,128)(2,1)} %copy.67), calls=%async_computation | async-start | bytes 9437184 | tf_op jit(solution)/shard_map/all_to_all | solution.py:238
  84.0 48.8 %all-to-all-done = bf16[4,1024,576]{1,2,0:T(8,128)(2,1)} async-done(((bf16[4,1024,576]{1,2,0:T(8,128)(2,1)}), bf16[4,1024,576]{1,2,0:T(8,128)(2,1)}, u32[]{:S(2)}, u32[]{:S(2)}) %all-to-all-start) | async-done | bytes 4718624 | tf_op jit(solution)/shard_map/all_to_all | solution.py:238
  132.8 7.7 %copy.68 = bf16[4,1024,576]{2,1,0:T(8,128)(2,1)} copy(bf16[4,1024,576]{1,2,0:T(8,128)(2,1)} %all-to-all-done) | data formatting | bytes 9437184 | tf_op jit(solution)/shard_map/all_to_all | solution.py:238
  140.5 21.2 %gather_fusion.1 = bf16[4096,576]{1,0:T(8,128)(2,1)} fusion(bf16[4096,576]{1,0:T(8,128)(2,1)} %bitcast.33, s32[4096]{0:T(1024)S(1)} %get-tuple-element.200), kind=kCustom, calls=%fused_computation.1.clone | custom fusion | bytes 9453568 | tf_op jit(solution)/shard_map/jit(_take)/gather | solution.py:114
  161.7 5.6 %select_select_fusion = bf16[4096,576]{1,0:T(8,128)(2,1)S(1)} fusion(bf16[4096,576]{1,0:T(8,128)(2,1)} %gather_fusion.1, pred[4096]{0:T(1024)(128)(4,1)S(1)} %compare_and_fusion.4, pred[4096]{0:T(1024)(128)(4,1)S(1)} %fusion.71), kind=kLoop, calls=%fused_computation.58 | loop fusion | flops 4718592 | bytes 9445376 | tf_op jit(solution)/shard_map/jit(_where)/select_n | solution.py:115
  167.8 1.8 copy-done
  173.0 67.8 %while.12 = (s32[]{:T(128)}, bf16[4096,128]{1,0:T(8,128)(2,1)S(1)}, s32[]{:T(128)}, s32[4096]{0:T(1024)S(1)}, bf16[4096,2,64]{0,2,1:T(8,128)(2,1)}, /*index=5*/b...) while((s32[]{:T(128)}, bf16[4096,128]{1,0:T(8,128)(2,1)S(1)}, ...), condition=%wide.region_12.14_spmd, body=%wide.region_9.13_spmd.sunk | while | flops 275909120 | bytes 10777831 | solution.py:154
  173.7 4.6 %fusion.112 = (f32[2,512]{1,0:T(2,128)S(1)}, f32[2,512,1024]{2,1,0:T(8,128)}) fusion(pred[512,1024]{1,0:T(8,128)(4,1)S(1)} %compare_and_fusion.7, bf16[4096,2,64]{0,2,1:T(8,128)(2,1)S(1)} %get-tuple-element.298, s32[]{:T(128)S(6)} %min.8, bf16[4096,2,64]{0,2,1:T(8,128)(2,1)} %get-tuple-element.297, s32[]{:T(128)S(6)} %select_n.445), kind=kOutput, calls=%fused_computation.236.clone.1 | convolution fusion | flops 138413056 | bytes 5115912 | tf_op jit(solution)/shard_map/while/body/sub | solution.py:142
  178.3 3.1 fusion.113
  182.2 4.6 %fusion.112 = (f32[2,512]{1,0:T(2,128)S(1)}, f32[2,512,1024]{2,1,0:T(8,128)}) fusion(pred[512,1024]{1,0:T(8,128)(4,1)S(1)} %compare_and_fusion.7, bf16[4096,2,64]{0,2,1:T(8,128)(2,1)S(1)} %get-tuple-element.298, s32[]{:T(128)S(6)} %min.8, bf16[4096,2,64]{0,2,1:T(8,128)(2,1)} %get-tuple-element.297, s32[]{:T(128)S(6)} %select_n.445), kind=kOutput, calls=%fused_computation.236.clone.1 | convolution fusion | flops 138413056 | bytes 5115912 | tf_op jit(solution)/shard_map/while/body/sub | solution.py:142
  186.7 3.2 fusion.113
  190.7 4.6 %fusion.112 = (f32[2,512]{1,0:T(2,128)S(1)}, f32[2,512,1024]{2,1,0:T(8,128)}) fusion(pred[512,1024]{1,0:T(8,128)(4,1)S(1)} %compare_and_fusion.7, bf16[4096,2,64]{0,2,1:T(8,128)(2,1)S(1)} %get-tuple-element.298, s32[]{:T(128)S(6)} %min.8, bf16[4096,2,64]{0,2,1:T(8,128)(2,1)} %get-tuple-element.297, s32[]{:T(128)S(6)} %select_n.445), kind=kOutput, calls=%fused_computation.236.clone.1 | convolution fusion | flops 138413056 | bytes 5115912 | tf_op jit(solution)/shard_map/while/body/sub | solution.py:142
  195.2 3.1 fusion.113
  199.1 4.6 %fusion.112 = (f32[2,512]{1,0:T(2,128)S(1)}, f32[2,512,1024]{2,1,0:T(8,128)}) fusion(pred[512,1024]{1,0:T(8,128)(4,1)S(1)} %compare_and_fusion.7, bf16[4096,2,64]{0,2,1:T(8,128)(2,1)S(1)} %get-tuple-element.298, s32[]{:T(128)S(6)} %min.8, bf16[4096,2,64]{0,2,1:T(8,128)(2,1)} %get-tuple-element.297, s32[]{:T(128)S(6)} %select_n.445), kind=kOutput, calls=%fused_computation.236.clone.1 | convolution fusion | flops 138413056 | bytes 5115912 | tf_op jit(solution)/shard_map/while/body/sub | solution.py:142
  203.7 3.1 fusion.113
  207.6 4.6 %fusion.112 = (f32[2,512]{1,0:T(2,128)S(1)}, f32[2,512,1024]{2,1,0:T(8,128)}) fusion(pred[512,1024]{1,0:T(8,128)(4,1)S(1)} %compare_and_fusion.7, bf16[4096,2,64]{0,2,1:T(8,128)(2,1)S(1)} %get-tuple-element.298, s32[]{:T(128)S(6)} %min.8, bf16[4096,2,64]{0,2,1:T(8,128)(2,1)} %get-tuple-element.297, s32[]{:T(128)S(6)} %select_n.445), kind=kOutput, calls=%fused_computation.236.clone.1 | convolution fusion | flops 138413056 | bytes 5115912 | tf_op jit(solution)/shard_map/while/body/sub | solution.py:142
  212.1 3.1 fusion.113
  216.0 4.6 %fusion.112 = (f32[2,512]{1,0:T(2,128)S(1)}, f32[2,512,1024]{2,1,0:T(8,128)}) fusion(pred[512,1024]{1,0:T(8,128)(4,1)S(1)} %compare_and_fusion.7, bf16[4096,2,64]{0,2,1:T(8,128)(2,1)S(1)} %get-tuple-element.298, s32[]{:T(128)S(6)} %min.8, bf16[4096,2,64]{0,2,1:T(8,128)(2,1)} %get-tuple-element.297, s32[]{:T(128)S(6)} %select_n.445), kind=kOutput, calls=%fused_computation.236.clone.1 | convolution fusion | flops 138413056 | bytes 5115912 | tf_op jit(solution)/shard_map/while/body/sub | solution.py:142
  220.6 3.1 fusion.113
  224.5 4.6 %fusion.112 = (f32[2,512]{1,0:T(2,128)S(1)}, f32[2,512,1024]{2,1,0:T(8,128)}) fusion(pred[512,1024]{1,0:T(8,128)(4,1)S(1)} %compare_and_fusion.7, bf16[4096,2,64]{0,2,1:T(8,128)(2,1)S(1)} %get-tuple-element.298, s32[]{:T(128)S(6)} %min.8, bf16[4096,2,64]{0,2,1:T(8,128)(2,1)} %get-tuple-element.297, s32[]{:T(128)S(6)} %select_n.445), kind=kOutput, calls=%fused_computation.236.clone.1 | convolution fusion | flops 138413056 | bytes 5115912 | tf_op jit(solution)/shard_map/while/body/sub | solution.py:142
  229.0 3.1 fusion.113
  232.9 4.6 %fusion.112 = (f32[2,512]{1,0:T(2,128)S(1)}, f32[2,512,1024]{2,1,0:T(8,128)}) fusion(pred[512,1024]{1,0:T(8,128)(4,1)S(1)} %compare_and_fusion.7, bf16[4096,2,64]{0,2,1:T(8,128)(2,1)S(1)} %get-tuple-element.298, s32[]{:T(128)S(6)} %min.8, bf16[4096,2,64]{0,2,1:T(8,128)(2,1)} %get-tuple-element.297, s32[]{:T(128)S(6)} %select_n.445), kind=kOutput, calls=%fused_computation.236.clone.1 | convolution fusion | flops 138413056 | bytes 5115912 | tf_op jit(solution)/shard_map/while/body/sub | solution.py:142
  237.5 3.1 fusion.113
  241.8 7.5 %all-to-all-start.2 = ((bf16[8,512,128]{2,1,0:T(8,128)(2,1)}), bf16[8,512,128]{2,1,0:T(8,128)(2,1)S(1)}, u32[]{:S(2)}, u32[]{:S(2)}) async-start(bf16[8,512,128]{2,1,0:T(8,128)(2,1)} %bitcast.41), calls=%async_computation.2 | async-start | bytes 2097152 | tf_op jit(solution)/shard_map/all_to_all | solution.py:255
  250.0 2.3 copy.69
  252.3 37.5 %all-to-all-done.2 = bf16[8,512,128]{2,1,0:T(8,128)(2,1)S(1)} async-done(((bf16[8,512,128]{2,1,0:T(8,128)(2,1)}), bf16[8,512,128]{2,1,0:T(8,128)(2,1)S(1)}, u32[]{:S(2)}, u32[]{:S(2)}) %all-to-all-start.2) | async-done | bytes 1048608 | tf_op jit(solution)/shard_map/all_to_all | solution.py:255
  289.8 4.3 all-to-all-start.1
  299.1 62.0 %all-to-all-done.1 = bf16[8,512,192]{1,2,0:T(8,128)(2,1)} async-done(((bf16[8,512,192]{1,2,0:T(8,128)(2,1)}), bf16[8,512,192]{1,2,0:T(8,128)(2,1)}, u32[]{:S(2)}, u32[]{:S(2)}) %all-to-all-start.1) | async-done | bytes 1572896 | tf_op jit(solution)/shard_map/all_to_all | solution.py:256
  361.2 1.8 convert_element_type.172
  363.0 2.3 copy.75
  365.3 5.1 %fusion.98 = (f32[512]{0:T(512)S(1)}, f32[512,1536]{1,0:T(8,128)S(1)}) fusion(f32[512,1536]{1,0:T(8,128)} %copy.75, bf16[512,1024]{0,1:T(8,128)(2,1)} %bitcast.46, bf16[1024,1536]{0,1:T(8,128)(2,1)} %all-gather.4.cloned.1.call-done), kind=kOutput, calls=%fused_computation.240 | convolution fusion | flops 1612185088 | bytes 10487808 | tf_op jit(solution)/shard_map/dot_general | solution.py:160
  371.1 7.7 %fusion.36 = f32[512,3072]{1,0:T(8,128)S(1)} fusion(bf16[1536,3072]{1,0:T(8,128)(2,1)} %all-gather.6.cloned.1.call-done, f32[512,1536]{1,0:T(8,128)S(1)} %get-tuple-element.207, f32[1536]{0:T(1024)S(1)} %copy-done.7, f32[1536]{0:T(1024)S(1)} %copy-done.8, f32[512]{0:T(512)S(1)} %add_rsqrt_fusion, f32[512]{0:T(512)S(1)} %broadcast_multiply_fusion), kind=kOutput, calls=%fused_computation.73 | convolution fusion | flops 4835770368 | bytes 18890752 | tf_op jit(solution)/shard_map/dot_general | solution.py:169
  380.9 4.3 collective-permute-start
  387.5 3.8 collective-permute-done.1
  391.2 55.4 %fusion.35 = bf16[512,1536]{1,0:T(8,128)(2,1)} fusion(f32[512,1536]{1,0:T(8,128)S(1)} %get-tuple-element.207, bf16[1536,1536]{0,1:T(8,128)(2,1)} %all-gather.8.cloned.1.call-done, pred[512]{0:T(512)(128)(4,1)} %get-tuple-element.176, bf16[512,1536]{1,0:T(8,128)(2,1)} %copy-done.2, bf16[15,1536]{1,0:T(8,128)(2,1)} %collective-permute-done.1, ...), kind=kOutput, calls=%fused_computation.72 | convolution fusion | flops 2590507008 | bytes 11320832 | tf_op jit(solution)/shard_map/dot_general | solution.py:265
  (104 shorter events, 26.1 us)
Async XLA Ops:
  6.5 358.8 %all-gather.4.cloned.1.call-start = ((), (), s32[]{:S(2)}) async-start(), calls=%async_computation.3 | async-start | bytes 3538944 | tf_op jit(solution)/shard_map/all_gather | solution.py:162
  7.3 363.7 %all-gather.6.cloned.1.call-start = ((), (), s32[]{:S(2)}) async-start(), calls=%async_computation.4 | async-start | bytes 10616832 | tf_op jit(solution)/shard_map/all_gather | solution.py:171
  31.2 5.4 %copy-start.6 = (s32[64]{0:T(128)S(1)}, s32[64]{0:T(128)}, u32[]{:S(2)}) copy-start(s32[64]{0:T(128)} %param.23) | copy-start | bytes 772
  31.2 5.5 %copy-start.5 = (s32[64]{0:T(128)S(1)}, s32[64]{0:T(128)}, u32[]{:S(2)}) copy-start(s32[64]{0:T(128)} %param.22) | copy-start | bytes 772
  76.5 56.2 %all-to-all-start = ((bf16[4,1024,576]{1,2,0:T(8,128)(2,1)}), bf16[4,1024,576]{1,2,0:T(8,128)(2,1)}, u32[]{:S(2)}, u32[]{:S(2)}) async-start(bf16[4,1024,576]{1,2,0:T(8,128)(2,1)} %copy.67), calls=%async_computation | async-start | bytes 9437184 | tf_op jit(solution)/shard_map/all_to_all | solution.py:238
  167.3 2.4 copy-start
  240.8 1.0 copy-start.1
  241.8 8.3 %slice-start = ((bf16[4096,576]{1,0:T(8,128)(2,1)}), bf16[4096,192]{1,0:T(8,128)(2,1)S(1)}, s32[]{:S(2)}) async-start(bf16[4096,576]{1,0:T(8,128)(2,1)} %copy-done), calls=%async_computation.6 | async-start | bytes 4194304 | tf_op jit(solution)/shard_map/slice | solution.py:253
  241.8 48.1 %all-to-all-start.2 = ((bf16[8,512,128]{2,1,0:T(8,128)(2,1)}), bf16[8,512,128]{2,1,0:T(8,128)(2,1)S(1)}, u32[]{:S(2)}, u32[]{:S(2)}) async-start(bf16[8,512,128]{2,1,0:T(8,128)(2,1)} %bitcast.41), calls=%async_computation.2 | async-start | bytes 2097152 | tf_op jit(solution)/shard_map/all_to_all | solution.py:255
  249.3 138.2 %all-gather.8.cloned.1.call-start = ((), (), s32[]{:S(2)}) async-start(), calls=%async_computation.5 | async-start | bytes 5308416 | tf_op jit(solution)/shard_map/all_gather | solution.py:267
  250.0 44.2 %copy-start.3 = (f32[31,1536]{1,0:T(8,128)S(1)}, f32[31,1536]{1,0:T(8,128)}, u32[]{:S(2)}) copy-start(f32[31,1536]{1,0:T(8,128)} %param.28) | copy-start | bytes 571396
  289.8 71.3 %all-to-all-start.1 = ((bf16[8,512,192]{1,2,0:T(8,128)(2,1)}), bf16[8,512,192]{1,2,0:T(8,128)(2,1)}, u32[]{:S(2)}, u32[]{:S(2)}) async-start(bf16[8,512,192]{1,2,0:T(8,128)(2,1)} %copy.69), calls=%async_computation.1 | async-start | bytes 3145728 | tf_op jit(solution)/shard_map/all_to_all | solution.py:256
  370.4 0.7 copy-start.7
  370.4 0.7 copy-start.8
  378.8 12.4 %copy-start.4 = (f32[1536]{0:T(1024)S(1)}, f32[1536]{0:T(1024)}, u32[]{:S(2)}) copy-start(f32[1536]{0:T(1024)} %get-tuple-element.119) | copy-start | bytes 18436
  379.7 1.2 copy-start.2
  380.9 6.6 %collective-permute-start = (bf16[15,1536]{1,0:T(8,128)(2,1)S(1)}, bf16[15,1536]{1,0:T(8,128)(2,1)}, u32[]{:S(2)}, u32[]{:S(2)}) collective-permute-start(bf16[15,1536]{1,0:T(8,128)(2,1)S(1)} %get-tuple-element.165), channel_id=1, source_target_pairs={{0,1},{1,2},{2,3},{3,4},{4,5},{5,6},{6,7},{8,9},{9,10},{10,11},{11... | collective-permute-start | bytes 138248 | tf_op jit(solution)/shard_map/ppermute | solution.py:24
  385.2 6.1 %collective-permute-start.1 = (bf16[15,1536]{1,0:T(8,128)(2,1)S(1)}, bf16[15,1536]{1,0:T(8,128)(2,1)}, u32[]{:S(2)}, u32[]{:S(2)}) collective-permute-start(bf16[15,1536]{1,0:T(8,128)(2,1)S(1)} %get-tuple-element.166), channel_id=1, source_target_pairs={{1,0},{2,1},{3,2},{4,3},{5,4},{6,5},{7,6},{9,8},{10,9},{11,10},{12... | collective-permute-start | bytes 138248 | tf_op jit(solution)/shard_map/ppermute | solution.py:26
Sparse Core Ops, SparseCore 0:
  9.5 61.2 all-gather.3
  72.8 136.4 all-gather.5
  252.3 116.2 all-gather.7
where the time goes:
time: 455 us; the launch traced here: 453 us
  waiting for transfers between devices  154 us (34%)
  matrix products  130 us (29%)
  local copies, waits for them, and re-layouts  103 us (23%)
  other arithmetic  28.5 us (6%)
  starting transfers between devices  22.8 us (5%)
  between operations  14.1 us (3%)
    all_to_all x1, waiting for transfers between devices, on_device(): lax.all_to_all(portion_carried, 'mp', split_axis=0, concat_axis=1, tiled=...  62 us
    dot_general x1, matrix products, on_device(): jnp.dot(swished, lax.all_gather(down_proj, 'mp', axis=1, tiled=True), pre...  55.4 us
    all_to_all x1, waiting for transfers between devices, on_device(): lax.all_to_all(pack_outgoing(stacked, send_frame, valid_slot), 'dp', spli...  48.8 us
    all_to_all x1, waiting for transfers between devices, on_device(): lax.all_to_all(context, 'mp', split_axis=0, concat_axis=1, tiled=True)  37.5 us
    sub x8, matrix products, attend_block(): exponentials = jnp.exp(scores - highest)  36.5 us
    dot_general x8, matrix products, attend_block(): jnp.einsum('hqk,khd->qhd', weights, value_block, preferred_element_type=j...  25.1 us
    gather x1, local copies, waits for them, and re-layouts, finalize_rows(): picked = jnp.take(received_rows, incoming_row, axis=0)  21.2 us
    gather x1, local copies, waits for them, and re-layouts, pack_outgoing(): picked = jnp.take(stacked, send_frame, axis=0)  21.2 us
  transfers between devices with their start and end apart: 8, of which 4 were waited for; matrix products, arithmetic and copies ran while one was open for 45% of the time, Pallas kernels for 0%

commit v1 on v0

--- a/solution.py
+++ b/solution.py
@@ -253,7 +253,12 @@
     portion_carried = balanced_rows[:, 3 * width_per_head :]
     context_slab, carried_slab = (
         lax.all_to_all(context, "mp", split_axis=0, concat_axis=1, tiled=True),
-        lax.all_to_all(portion_carried, "mp", split_axis=0, concat_axis=1, tiled=True),
+        jnp.concatenate(
+            lax.all_to_all(
+                jnp.stack(jnp.split(portion_carried, lax.axis_size("mp"), axis=0)), "mp", 0, 0
+            ),
+            axis=1,
+        ),
     )
     carried, gated_rows = front(
         context_slab, carried_slab, out_proj, norm_gain, norm_bias, glu_proj

time: 455 us -> 437 us (0.960)
  waiting for transfers between devices: 154 us -> 132 us
  local copies, waits for them, and re-layouts: 103 us -> 115 us
  matrix products: 130 us -> 123 us
    all_to_all x1, waiting for transfers between devices: 62 us -> 45.2 us  [on_device(): lax.all_to_all(jnp.stack(jnp.split(portion_carried, lax.axis_size('mp'),...]
    sub x8, matrix products: 36.5 us -> 29.2 us  [attend_block(): exponentials = jnp.exp(scores - highest)]
    unnamed x21 -> x26, local copies, waits for them, and re-layouts: 14 us -> 19.8 us
    dynamic_update_slice x16, local copies, waits for them, and re-layouts: 1.16 us -> 6.27 us  [attend_block(): lax.dynamic_update_slice_in_dim(context, blended.reshape(QBLK, width_per_...]
  transfers between devices with their start and end apart: 8 -> 8, of which waited for: 4 -> 4; matrix products, arithmetic and copies ran while one was open for 45% -> 48% of each run, Pallas kernels for 0% -> 0%
where the time goes in v1:
time: 437 us; the launch traced here: 435 us
  waiting for transfers between devices  132 us (30%)
  matrix products  123 us (28%)
  local copies, waits for them, and re-layouts  115 us (26%)
  other arithmetic  28.5 us (7%)
  starting transfers between devices  21.9 us (5%)
  between operations  14.1 us (3%)
    dot_general x1, matrix products, on_device(): jnp.dot(swished, lax.all_gather(down_proj, 'mp', axis=1, tiled=True), pre...  55.4 us
    all_to_all x1, waiting for transfers between devices, on_device(): lax.all_to_all(pack_outgoing(stacked, send_frame, valid_slot), 'dp', spli...  48.1 us
    all_to_all x1, waiting for transfers between devices, on_device(): lax.all_to_all(jnp.stack(jnp.split(portion_carried, lax.axis_size('mp'),...  45.2 us
    all_to_all x1, waiting for transfers between devices, on_device(): lax.all_to_all(context, 'mp', split_axis=0, concat_axis=1, tiled=True)  33.1 us
    sub x8, matrix products, attend_block(): exponentials = jnp.exp(scores - highest)  29.2 us
    dot_general x8, matrix products, attend_block(): jnp.einsum('hqk,khd->qhd', weights, value_block, preferred_element_type=j...  25.3 us
    gather x1, local copies, waits for them, and re-layouts, finalize_rows(): picked = jnp.take(received_rows, incoming_row, axis=0)  21.2 us
    gather x1, local copies, waits for them, and re-layouts, pack_outgoing(): picked = jnp.take(stacked, send_frame, axis=0)  21.2 us
  transfers between devices with their start and end apart: 8, of which 4 were waited for; matrix products, arithmetic and copies ran while one was open for 48% of the time, Pallas kernels for 0%

profile of v1, /device:TPU:4, one launch (start us, length us, event | category | flops | bytes accessed | tf_op | source)
XLA Modules:
  0.0 435.0 jit_solution(17416700312984460316)
XLA Ops:
  8.0 2.4 copy.61
  10.5 1.5 copy.62
  13.0 3.7 copy.63
  16.7 4.5 %copy.64 = bf16[2048,2,2,64]{3,2,1,0:T(2,128)(2,1)S(1)} copy(bf16[2048,2,2,64]{0,3,1,2:T(8,128)(2,1)} %bitcast.68) | data formatting | bytes 2097152 | tf_op jit(solution)/shard_map/transpose | solution.py:38
  21.2 1.8 reshape.218
  23.0 3.7 copy.65
  26.7 4.5 %copy.66 = bf16[2048,2,2,64]{3,2,1,0:T(2,128)(2,1)S(1)} copy(bf16[2048,2,2,64]{0,3,1,2:T(8,128)(2,1)} %bitcast.69) | data formatting | bytes 2097152 | tf_op jit(solution)/shard_map/transpose | solution.py:38
  31.2 1.8 reshape.220
  33.0 3.6 reshape_transpose_reshape.3
  37.2 4.5 %pad_maximum_fusion = bf16[4096,576]{1,0:T(8,128)(2,1)} fusion(bf16[4096,192]{1,0:T(8,128)(2,1)S(1)} %reshape_transpose_reshape.3, bf16[4096,128]{1,0:T(8,128)(2,1)} %reshape.220, bf16[4096,128]{1,0:T(8,128)(2,1)} %reshape.218, bf16[4096,128]{1,0:T(8,128)(2,1)S(1)} %reshape.216), kind=kLoop, calls=%fused_computation.57 | loop fusion | flops 18874368 | bytes 9437184 | tf_op jit(solution)/shard_map/concatenate | solution.py:237
  41.7 21.2 %gather_fusion = bf16[4096,576]{1,0:T(8,128)(2,1)} fusion(bf16[4096,576]{1,0:T(8,128)(2,1)} %pad_maximum_fusion, s32[4096]{0:T(1024)S(1)} %fusion.88), kind=kCustom, calls=%fused_computation.clone | custom fusion | bytes 9453568 | tf_op jit(solution)/shard_map/jit(_take)/gather | solution.py:109
  63.0 5.8 %select_select_fusion.1 = bf16[4096,576]{1,0:T(8,128)(2,1)} fusion(bf16[4096,576]{1,0:T(8,128)(2,1)} %gather_fusion, pred[4096]{0:T(1024)(128)(4,1)S(1)} %compare_and_fusion.5, pred[4096]{0:T(1024)(128)(4,1)S(1)} %fusion.93), kind=kLoop, calls=%fused_computation.59 | loop fusion | flops 4718592 | bytes 9445376 | tf_op jit(solution)/shard_map/jit(_where)/select_n | solution.py:110
  68.9 7.7 %copy.67 = bf16[4,1024,576]{1,2,0:T(8,128)(2,1)} copy(bf16[4,1024,576]{2,1,0:T(8,128)(2,1)} %bitcast.65) | data formatting | bytes 9437184 | tf_op jit(solution)/shard_map/all_to_all | solution.py:238
  76.5 5.1 %all-to-all-start = ((bf16[4,1024,576]{1,2,0:T(8,128)(2,1)}), bf16[4,1024,576]{1,2,0:T(8,128)(2,1)}, u32[]{:S(2)}, u32[]{:S(2)}) async-start(bf16[4,1024,576]{1,2,0:T(8,128)(2,1)} %copy.67), calls=%async_computation | async-start | bytes 9437184 | tf_op jit(solution)/shard_map/all_to_all | solution.py:238
  84.7 48.1 %all-to-all-done = bf16[4,1024,576]{1,2,0:T(8,128)(2,1)} async-done(((bf16[4,1024,576]{1,2,0:T(8,128)(2,1)}), bf16[4,1024,576]{1,2,0:T(8,128)(2,1)}, u32[]{:S(2)}, u32[]{:S(2)}) %all-to-all-start) | async-done | bytes 4718624 | tf_op jit(solution)/shard_map/all_to_all | solution.py:238
  132.8 7.7 %copy.68 = bf16[4,1024,576]{2,1,0:T(8,128)(2,1)} copy(bf16[4,1024,576]{1,2,0:T(8,128)(2,1)} %all-to-all-done) | data formatting | bytes 9437184 | tf_op jit(solution)/shard_map/all_to_all | solution.py:238
  140.5 21.2 %gather_fusion.1 = bf16[4096,576]{1,0:T(8,128)(2,1)} fusion(bf16[4096,576]{1,0:T(8,128)(2,1)} %bitcast.64, s32[4096]{0:T(1024)S(1)} %get-tuple-element.200), kind=kCustom, calls=%fused_computation.1.clone | custom fusion | bytes 9453568 | tf_op jit(solution)/shard_map/jit(_take)/gather | solution.py:114
  161.7 5.6 %select_select_fusion = bf16[4096,576]{1,0:T(8,128)(2,1)S(1)} fusion(bf16[4096,576]{1,0:T(8,128)(2,1)} %gather_fusion.1, pred[4096]{0:T(1024)(128)(4,1)S(1)} %compare_and_fusion.4, pred[4096]{0:T(1024)(128)(4,1)S(1)} %fusion.79), kind=kLoop, calls=%fused_computation.58 | loop fusion | flops 4718592 | bytes 9445376 | tf_op jit(solution)/shard_map/jit(_where)/select_n | solution.py:115
  167.8 1.8 copy-done
  173.2 65.5 %while.12 = (s32[]{:T(128)}, bf16[4096,128]{1,0:T(8,128)(2,1)}, s32[]{:T(128)}, s32[4096]{0:T(1024)S(1)}, bf16[4096,2,64]{0,2,1:T(8,128)(2,1)}, /*index=5*/bf16[...) while((s32[]{:T(128)}, bf16[4096,128]{1,0:T(8,128)(2,1)}, ...), condition=%wide.region_12.14_spmd, body=%wide.region_9.13_spmd.sunk | while | flops 275909120 | bytes 10777831 | solution.py:154
  173.7 3.7 fusion.120
  177.4 3.1 fusion.121
  181.9 3.7 fusion.120
  185.5 3.2 fusion.121
  190.1 3.7 fusion.120
  193.8 3.1 fusion.121
  198.2 3.7 fusion.120
  201.9 3.1 fusion.121
  206.4 3.7 fusion.120
  210.0 3.1 fusion.121
  214.5 3.7 fusion.120
  218.2 3.3 fusion.121
  222.9 3.7 fusion.120
  226.5 3.2 fusion.121
  231.0 3.7 fusion.120
  234.7 3.1 fusion.121
  238.6 7.1 %all-to-all-start.2 = ((bf16[8,512,128]{2,1,0:T(8,128)(2,1)}), bf16[8,512,128]{2,1,0:T(8,128)(2,1)S(1)}, u32[]{:S(2)}, u32[]{:S(2)}) async-start(bf16[8,512,128]{2,1,0:T(8,128)(2,1)} %bitcast.23), calls=%async_computation.2 | async-start | bytes 2097152 | tf_op jit(solution)/shard_map/all_to_all | solution.py:255
  253.5 2.3 copy.69
  255.8 33.1 %all-to-all-done.2 = bf16[8,512,128]{2,1,0:T(8,128)(2,1)S(1)} async-done(((bf16[8,512,128]{2,1,0:T(8,128)(2,1)}), bf16[8,512,128]{2,1,0:T(8,128)(2,1)S(1)}, u32[]{:S(2)}, u32[]{:S(2)}) %all-to-all-start.2) | async-done | bytes 1048608 | tf_op jit(solution)/shard_map/all_to_all | solution.py:255
  288.9 4.3 all-to-all-start.1
  298.3 45.2 %all-to-all-done.1 = bf16[8,512,192]{1,2,0:T(8,128)(2,1)} async-done(((bf16[8,512,192]{1,2,0:T(8,128)(2,1)}), bf16[8,512,192]{1,2,0:T(8,128)(2,1)}, u32[]{:S(2)}, u32[]{:S(2)}) %all-to-all-start.1) | async-done | bytes 1572896 | tf_op jit(solution)/shard_map/all_to_all | solution.py:257
  343.5 1.8 convert_element_type.172
  345.3 2.3 copy.75
  347.6 5.1 %fusion.106 = (f32[512]{0:T(512)S(1)}, f32[512,1536]{1,0:T(8,128)S(1)}) fusion(f32[512,1536]{1,0:T(8,128)} %copy.75, bf16[512,1024]{0,1:T(8,128)(2,1)} %bitcast.75, bf16[1024,1536]{0,1:T(8,128)(2,1)} %all-gather.4.cloned.1.call-done), kind=kOutput, calls=%fused_computation.256 | convolution fusion | flops 1612185088 | bytes 10487808 | tf_op jit(solution)/shard_map/dot_general | solution.py:160
  353.4 7.7 %fusion.36 = f32[512,3072]{1,0:T(8,128)S(1)} fusion(bf16[1536,3072]{1,0:T(8,128)(2,1)} %all-gather.6.cloned.1.call-done, f32[512,1536]{1,0:T(8,128)S(1)} %get-tuple-element.207, f32[1536]{0:T(1024)S(1)} %copy-done.6, f32[1536]{0:T(1024)S(1)} %copy-done.7, f32[512]{0:T(512)S(1)} %add_rsqrt_fusion, f32[512]{0:T(512)S(1)} %broadcast_multiply_fusion), kind=kOutput, calls=%fused_computation.73 | convolution fusion | flops 4835770368 | bytes 18890752 | tf_op jit(solution)/shard_map/dot_general | solution.py:169
  363.2 3.8 collective-permute-start
  369.3 3.8 collective-permute-done.1
  373.1 55.4 %fusion.35 = bf16[512,1536]{1,0:T(8,128)(2,1)} fusion(f32[512,1536]{1,0:T(8,128)S(1)} %get-tuple-element.207, bf16[1536,1536]{0,1:T(8,128)(2,1)} %all-gather.8.cloned.1.call-done, pred[512]{0:T(512)(128)(4,1)} %get-tuple-element.176, bf16[512,1536]{1,0:T(8,128)(2,1)} %copy-done.1, bf16[15,1536]{1,0:T(8,128)(2,1)} %collective-permute-done.1, ...), kind=kOutput, calls=%fused_computation.72 | convolution fusion | flops 2590507008 | bytes 11320832 | tf_op jit(solution)/shard_map/dot_general | solution.py:270
  (108 shorter events, 38.2 us)
Async XLA Ops:
  6.5 341.1 %all-gather.4.cloned.1.call-start = ((), (), s32[]{:S(2)}) async-start(), calls=%async_computation.3 | async-start | bytes 3538944 | tf_op jit(solution)/shard_map/all_gather | solution.py:162
  7.3 346.0 %all-gather.6.cloned.1.call-start = ((), (), s32[]{:S(2)}) async-start(), calls=%async_computation.4 | async-start | bytes 10616832 | tf_op jit(solution)/shard_map/all_gather | solution.py:171
  31.2 5.4 %copy-start.5 = (s32[64]{0:T(128)S(1)}, s32[64]{0:T(128)}, u32[]{:S(2)}) copy-start(s32[64]{0:T(128)} %param.23) | copy-start | bytes 772
  31.2 5.5 %copy-start.4 = (s32[64]{0:T(128)S(1)}, s32[64]{0:T(128)}, u32[]{:S(2)}) copy-start(s32[64]{0:T(128)} %param.22) | copy-start | bytes 772
  76.5 56.2 %all-to-all-start = ((bf16[4,1024,576]{1,2,0:T(8,128)(2,1)}), bf16[4,1024,576]{1,2,0:T(8,128)(2,1)}, u32[]{:S(2)}, u32[]{:S(2)}) async-start(bf16[4,1024,576]{1,2,0:T(8,128)(2,1)} %copy.67), calls=%async_computation | async-start | bytes 9437184 | tf_op jit(solution)/shard_map/all_to_all | solution.py:238
  81.6 287.7 %all-gather.8.cloned.1.call-start = ((), (), s32[]{:S(2)}) async-start(), calls=%async_computation.5 | async-start | bytes 5308416 | tf_op jit(solution)/shard_map/all_gather | solution.py:272
  167.3 2.4 copy-start
  238.6 50.3 %all-to-all-start.2 = ((bf16[8,512,128]{2,1,0:T(8,128)(2,1)}), bf16[8,512,128]{2,1,0:T(8,128)(2,1)S(1)}, u32[]{:S(2)}, u32[]{:S(2)}) async-start(bf16[8,512,128]{2,1,0:T(8,128)(2,1)} %bitcast.23), calls=%async_computation.2 | async-start | bytes 2097152 | tf_op jit(solution)/shard_map/all_to_all | solution.py:255
  253.5 39.8 %copy-start.2 = (f32[31,1536]{1,0:T(8,128)S(1)}, f32[31,1536]{1,0:T(8,128)}, u32[]{:S(2)}) copy-start(f32[31,1536]{1,0:T(8,128)} %param.28) | copy-start | bytes 571396
  288.9 54.6 %all-to-all-start.1 = ((bf16[8,512,192]{1,2,0:T(8,128)(2,1)}), bf16[8,512,192]{1,2,0:T(8,128)(2,1)}, u32[]{:S(2)}, u32[]{:S(2)}) async-start(bf16[8,512,192]{1,2,0:T(8,128)(2,1)} %copy.69), calls=%async_computation.1 | async-start | bytes 3145728 | tf_op jit(solution)/shard_map/all_to_all | solution.py:257
  352.7 0.7 copy-start.6
  352.7 0.7 copy-start.7
  361.1 11.9 %copy-start.3 = (f32[1536]{0:T(1024)S(1)}, f32[1536]{0:T(1024)}, u32[]{:S(2)}) copy-start(f32[1536]{0:T(1024)} %get-tuple-element.119) | copy-start | bytes 18436
  362.0 1.2 copy-start.1
  363.2 6.1 %collective-permute-start = (bf16[15,1536]{1,0:T(8,128)(2,1)S(1)}, bf16[15,1536]{1,0:T(8,128)(2,1)}, u32[]{:S(2)}, u32[]{:S(2)}) collective-permute-start(bf16[15,1536]{1,0:T(8,128)(2,1)S(1)} %get-tuple-element.165), channel_id=1, source_target_pairs={{0,1},{1,2},{2,3},{3,4},{4,5},{5,6},{6,7},{8,9},{9,10},{10,11},{11... | collective-permute-start | bytes 138248 | tf_op jit(solution)/shard_map/ppermute | solution.py:24
  367.0 6.1 %collective-permute-start.1 = (bf16[15,1536]{1,0:T(8,128)(2,1)S(1)}, bf16[15,1536]{1,0:T(8,128)(2,1)}, u32[]{:S(2)}, u32[]{:S(2)}) collective-permute-start(bf16[15,1536]{1,0:T(8,128)(2,1)S(1)} %get-tuple-element.166), channel_id=1, source_target_pairs={{1,0},{2,1},{3,2},{4,3},{5,4},{6,5},{7,6},{9,8},{10,9},{11,10},{12... | collective-permute-start | bytes 138248 | tf_op jit(solution)/shard_map/ppermute | solution.py:26
Sparse Core Ops, SparseCore 0:
  9.5 61.2 all-gather.3
  72.8 136.4 all-gather.5
  211.5 124.2 all-gather.7
